TPU v7x, 512 devices: a whole 4x8x8 slice. The times are simulated.
512 devices in a mesh: row: 64 (over z, y), col: 8 (over x, core).
Axes of the slice: x: 4, y: 8, z: 8, core: 2. Of those that a mesh axis runs over, the one named last changes fastest.
Arguments:
- dinv0: bfloat16 [65536, 4096], P('row', 'col'), as said below
- dinv1: bfloat16 [32768, 4096], P('row', 'col'), as said below
- dinv2: bfloat16 [16384, 4096], P('row', 'col'), as said below
- offdiag0: bfloat16 [65536, 4096], P('row', 'col'), may hold values from -0.0625 to 0.0625
- offdiag1: bfloat16 [32768, 4096], P('row', 'col'), may hold values from -0.0625 to 0.0625
- rhs0: bfloat16 [65536, 128], P(('row', 'col')), may hold values from -6 to 6
- rhs1: bfloat16 [32768, 128], P(('row', 'col')), may hold values from -6 to 6
- rhs2: bfloat16 [16384, 128], P(('row', 'col')), may hold values from -6 to 6
- block_rows0: int32 [16, 64, 16], replicated, may hold values from 0 to 63, all different within a row
- block_rows1: int32 [8, 64, 16], replicated, may hold values from 0 to 63, all different within a row
Outputs:
- solution0: float32 [65536, 128], P(('row', 'col'))
- solution1: float32 [32768, 128], P(('row', 'col'))
- solution2: float32 [16384, 128], P(('row', 'col'))
Inputs may be any that keep to these rules, and one draw needn't show every extreme that they name: `block_rows0`: each row of the last dimension lists 16 different block rows. `block_rows1`: each row of the last dimension lists 16 different block rows. `dinv0`: each supernode's block is lower triangular in global order, with a positive diagonal. `dinv1`: each supernode's block is lower triangular in global order, with a positive diagonal. `dinv2`: each supernode's block is lower triangular in global order, with a positive diagonal.
All inputs are finite; a program needn't handle non-finite values.
Results may differ from a plain program's by a relative error of at most 0.0095.
Values may be sent and summed in bfloat16 or wider, within the bound.
No kernel may reach another device: no remote copies, remote signals or barrier semaphores. Data moves between devices by JAX's collectives and lax.ppermute only.
A program may use at most 64 MiB of HBM per device.

v0:
```python
import jax
import jax.numpy as jnp
from jax import lax
from jax.sharding import PartitionSpec as P

MB = 64
GR = 4


def partner(value, axis, stride):
    return lax.ppermute(value, axis, [(i, i ^ 1 << stride) for i in range(lax.axis_size(axis))])


def own_bit(which):
    return lax.axis_index("row") >> which & 1


def row_join(pieces, depth):
    joined = pieces
    for which in range(depth):
        other = partner(joined, "row", which)
        first = jnp.concatenate((joined, other), axis=1)
        second = jnp.concatenate((other, joined), axis=1)
        joined = jnp.where(own_bit(which) == 0, first, second)
    return joined.reshape(-1, joined.shape[-1])


def row_fold(partial_value, row_blocks, depth):
    width = partial_value.shape[-1]
    folded = partial_value.reshape(row_blocks, 1 << depth, -1, width)
    for which in range(depth):
        halves = folded.reshape(row_blocks, folded.shape[1] // 2, 2, folded.shape[2], width)
        mine = own_bit(which)
        keeping = lax.dynamic_index_in_dim(halves, mine, 2, keepdims=False)
        sending = lax.dynamic_index_in_dim(halves, 1 - mine, 2, keepdims=False)
        folded = keeping + partner(sending.astype(jnp.bfloat16), "row", which).astype(sending.dtype)
    return folded


def column_sum(partial_value, col_devs):
    width = partial_value.shape[-1]
    shaped = partial_value.reshape(-1, col_devs, MB // col_devs, width)
    return lax.psum_scatter(shaped, "col", scatter_dimension=1, tiled=True)


def column_join(pieces):
    gathered = lax.all_gather(pieces, "col", axis=1, tiled=True)
    return gathered.reshape(-1, gathered.shape[-1])


def sibling_fold(values, which):
    mine = own_bit(which)
    keeping = lax.dynamic_index_in_dim(values, mine, 1, keepdims=True)
    sending = lax.dynamic_index_in_dim(values, 1 - mine, 1, keepdims=True)
    return keeping + partner(sending.astype(jnp.bfloat16), "row", which).astype(sending.dtype)


def parent_rows(values, which):
    other = partner(values, "row", which)
    first = jnp.concatenate((values, other), axis=1)
    second = jnp.concatenate((other, values), axis=1)
    joined = jnp.where(own_bit(which) == 0, first, second)
    return joined.reshape(joined.shape[0] * 2, 1, joined.shape[2], joined.shape[3])


def coupling(values, listings, depth):
    row_count = values.shape[0]
    row_blocks = row_count // MB
    group = 1 << depth
    position = lax.axis_index("row")
    member = position // group
    local = position % group
    owned = jnp.arange(row_blocks, dtype=jnp.int32) * group + local
    listing = lax.dynamic_index_in_dim(listings, member, 0, keepdims=False)
    listed = jnp.any(listing[None, :, :] == owned[:, None, None], axis=-1)
    unit_width = values.shape[1] // listed.shape[1]
    keeping = jnp.repeat(jnp.repeat(listed, MB, axis=0), unit_width, axis=1)
    return jnp.where(keeping, values, jnp.zeros_like(values))


def per_device(dinv0, dinv1, dinv2, offdiag0, offdiag1, rhs0, rhs1, rhs2, block_rows0, block_rows1):
    col_devs = lax.axis_size("col")
    col_width = MB // col_devs
    width = rhs0.shape[1]
    lowest = GR.bit_length() - 1
    depths = (lowest, lowest + 1, lowest + 2)
    inverses = (dinv0, dinv1, dinv2)
    couplings = (
        coupling(offdiag0, block_rows0, depths[0]),
        coupling(offdiag1, block_rows1, depths[1]),
    )
    sides = (rhs0, rhs1, rhs2)

    def as_pieces(values):
        return values.reshape(-1, 1, col_width, width)

    solved = []
    residual = as_pieces(rhs0)
    for level in range(3):
        column_form = row_join(residual, depths[level])
        product = jnp.dot(inverses[level], column_form, preferred_element_type=jnp.float32)
        solved_pieces = column_sum(product, col_devs).astype(jnp.bfloat16)
        solved.append(solved_pieces)
        if level < 2:
            solved_columns = row_join(solved_pieces, depths[level])
            partial_value = jnp.dot(
                couplings[level], solved_columns, preferred_element_type=jnp.float32
            )
            summed = column_sum(partial_value, col_devs)
            summed = summed.reshape(summed.shape[0] // 2, 2, col_width, width)
            update = sibling_fold(summed, depths[level])
            residual = (as_pieces(sides[level + 1]).astype(jnp.float32) - update).astype(
                jnp.bfloat16
            )
    outputs = [None, None, None]
    weighted = solved[2]
    for level in (2, 1, 0):
        row_form = column_join(weighted)
        product = jnp.einsum(
            "ij,in->jn", inverses[level], row_form, preferred_element_type=jnp.float32
        )
        answer = row_fold(product, row_form.shape[0] // MB, depths[level])
        outputs[level] = answer.reshape(-1, width)
        if level > 0:
            child_pieces = parent_rows(answer.astype(jnp.bfloat16), depths[level - 1])
            child_form = column_join(child_pieces)
            partial_value = jnp.einsum(
                "ij,in->jn", couplings[level - 1], child_form, preferred_element_type=jnp.float32
            )
            carried = row_fold(partial_value, child_form.shape[0] // MB, depths[level - 1])
            weighted = (solved[level - 1].astype(jnp.float32) - carried).astype(jnp.bfloat16)
    return (outputs[0], outputs[1], outputs[2])


def solution(mesh):
    placed = (
        P("row", "col"),
        P("row", "col"),
        P("row", "col"),
        P("row", "col"),
        P("row", "col"),
        P(("row", "col"), None),
        P(("row", "col"), None),
        P(("row", "col"), None),
        P(),
        P(),
    )
    return jax.shard_map(
        per_device,
        mesh=mesh,
        in_specs=placed,
        out_specs=(P(("row", "col"), None), P(("row", "col"), None), P(("row", "col"), None)),
        check_vma=False,
    )
```

profile of v0, /device:TPU:24, one launch (start us, length us, event | category | flops | bytes accessed | tf_op | source)
XLA Modules:
  0.0 549.9 jit_solution(3072285865795595267)
XLA Ops:
  7.2 2.5 collective-permute-start
  13.4 6.0 %collective-permute-start.1 = (bf16[16,2,8,128]{3,2,1,0:T(8,128)(2,1)S(1)}, bf16[16,2,8,128]{3,2,1,0:T(8,128)(2,1)S(1)}, u32[]{:S(2)}, u32[]{:S(2)}) collective-permute-start(bf16[16,2,8,128]{3,2,1,0:T(8,128)(2,1)S(1)} %maximum_select_fusion.5), channel_id=1, source_target_pairs={{0,16},{8,24},{16,0},{24,8},{32,48},{40,56},{48,32},{56,40},{64,80... | collective-permute-start | bytes 196616 | tf_op jit(solution)/shard_map/ppermute | solution.py:11
  19.4 2.2 collective-permute-done.1
  22.4 29.2 %all-reduce.14 = bf16[16,8,8,128]{3,2,1,0:T(8,128)(2,1)S(1)} all-reduce(f32[16,8,8,128]{3,2,1,0:T(8,128)S(1)} %bitcast.169), channel_id=2, replica_groups=mesh['row'=64,'col'=8] {'col'}, use_global_device_ids=true, to_apply=%region_0.1.clone | all-reduce | flops 131072 | bytes 786432
  52.2 4.1 collective-permute-start.2
  58.5 4.8 collective-permute-start.3
  66.9 73.2 %all-reduce.11.cloned.1.call-done = f32[16,8,8,128]{3,2,1,0:T(8,128)} async-done(((f32[16,8,8,128]{3,2,1,0:T(8,128)}), f32[16,8,8,128]{3,2,1,0:T(8,128)}) %all-reduce.11.cloned.1.call-update) | async-done | bytes 524304
  141.6 4.7 collective-permute-start.4
  146.2 4.9 collective-permute-done.4
  151.1 2.6 collective-permute-start.5
  153.7 3.0 collective-permute-done.5
  156.8 2.4 collective-permute-start.6
  159.2 4.3 collective-permute-done.6
  163.5 4.8 collective-permute-start.7
  169.0 4.6 collective-permute-done.7
  174.0 26.3 %all-reduce.15 = bf16[8,8,8,128]{3,2,1,0:T(8,128)(2,1)S(1)} all-reduce(f32[8,8,8,128]{3,2,1,0:T(8,128)S(1)} %bitcast.170), channel_id=4, replica_groups=mesh['row'=64,'col'=8] {'col'}, use_global_device_ids=true, to_apply=%region_3.4.clone | all-reduce | flops 65536 | bytes 393216
  201.0 3.4 collective-permute-start.8
  204.4 2.2 collective-permute-done.8
  206.6 2.5 collective-permute-start.9
  209.6 2.1 copy.79
  213.3 5.6 %collective-permute-start.10 = (bf16[8,4,8,128]{3,2,1,0:T(8,128)(2,1)S(1)}, bf16[8,4,8,128]{3,2,1,0:T(8,128)(2,1)S(1)}, u32[]{:S(2)}, u32[]{:S(2)}) collective-permute-start(bf16[8,4,8,128]{3,2,1,0:T(8,128)(2,1)S(1)} %maximum_select_fusion.8), channel_id=1, source_target_pairs={{0,32},{8,40},{16,48},{24,56},{32,0},{40,8},{48,16},{56,24},{64,96... | collective-permute-start | bytes 196616 | tf_op jit(solution)/shard_map/ppermute | solution.py:11
  221.1 2.3 collective-permute-done.10
  225.5 72.1 %all-reduce.13.cloned.1.call-done = f32[8,8,8,128]{3,2,1,0:T(8,128)} async-done(((f32[8,8,8,128]{3,2,1,0:T(8,128)}), f32[8,8,8,128]{3,2,1,0:T(8,128)}) %all-reduce.13.cloned.1.call-update) | async-done | bytes 262160
  299.0 3.7 collective-permute-start.11
  304.7 2.6 collective-permute-start.12
  307.3 3.1 collective-permute-done.12
  310.4 2.4 collective-permute-start.13
  312.8 4.3 collective-permute-done.13
  317.1 4.5 collective-permute-start.14
  321.6 5.2 collective-permute-done.14
  326.8 3.6 collective-permute-start.15
  330.4 2.6 collective-permute-done.15
  334.9 25.3 %all-reduce.16 = bf16[4,8,8,128]{3,2,1,0:T(8,128)(2,1)} all-reduce(f32[4,8,8,128]{3,2,1,0:T(8,128)S(1)} %bitcast.183), channel_id=6, replica_groups=mesh['row'=64,'col'=8] {'col'}, use_global_device_ids=true, to_apply=%region_6.7.clone | all-reduce | flops 32768 | bytes 196608
  361.5 11.2 %all_gather.15 = bf16[4,8,8,128]{3,2,1,0:T(8,128)(2,1)S(1)} all-gather(bf16[4,1,8,128]{3,2,1,0:T(8,128)(2,1)S(1)} %dynamic-slice_convert_fusion.14), channel_id=1, replica_groups=mesh['row'=64,'col'=8] {'col'}, dimensions={1}, use_global_device_ids=true | all-gather | bytes 73728 | tf_op jit(solution)/shard_map/all_gather | solution.py:47
  374.7 2.7 collective-permute-start.16
  377.4 3.6 collective-permute-done.16
  381.9 2.3 collective-permute-start.17
  384.2 4.8 collective-permute-done.17
  389.0 4.2 collective-permute-start.18
  393.2 5.4 collective-permute-done.18
  398.6 3.6 collective-permute-start.19
  404.7 3.5 collective-permute-start.20
  410.3 11.3 %all_gather.16 = bf16[8,8,8,128]{3,2,1,0:T(8,128)(2,1)S(1)} all-gather(bf16[8,1,8,128]{3,2,1,0:T(8,128)(2,1)S(1)} %bitcast.201), channel_id=1, replica_groups=mesh['row'=64,'col'=8] {'col'}, dimensions={1}, use_global_device_ids=true | all-gather | bytes 147456 | tf_op jit(solution)/shard_map/all_gather | solution.py:47
  421.9 2.4 collective-permute-start.21
  424.4 3.8 collective-permute-done.21
  430.1 5.1 collective-permute-done.22
  435.3 3.9 collective-permute-start.23
  439.1 5.7 %collective-permute-done.23 = bf16[8,1,8,128]{3,2,1,0:T(8,128)(2,1)S(1)} collective-permute-done((bf16[8,1,8,128]{3,2,1,0:T(8,128)(2,1)S(1)}, bf16[8,1,8,128]{3,2,1,0:T(8,128)(2,1)S(1)}, u32[]{:S(2)}, u32[]{:S(2)}) %collective-permute-start.23) | collective-permute-done | bytes 16416 | tf_op jit(solution)/shard_map/ppermute | solution.py:11
  446.2 11.3 %all_gather.17 = bf16[8,8,8,128]{3,2,1,0:T(8,128)(2,1)S(1)} all-gather(bf16[8,1,8,128]{3,2,1,0:T(8,128)(2,1)S(1)} %subtract_convert_fusion.1), channel_id=1, replica_groups=mesh['row'=64,'col'=8] {'col'}, dimensions={1}, use_global_device_ids=true | all-gather | bytes 147456 | tf_op jit(solution)/shard_map/all_gather | solution.py:47
  457.9 2.2 collective-permute-start.24
  460.0 4.1 collective-permute-done.24
  466.1 4.9 collective-permute-done.25
  471.0 3.8 collective-permute-start.26
  474.8 5.8 %collective-permute-done.26 = bf16[8,1,8,128]{3,2,1,0:T(8,128)(2,1)S(1)} collective-permute-done((bf16[8,1,8,128]{3,2,1,0:T(8,128)(2,1)S(1)}, bf16[8,1,8,128]{3,2,1,0:T(8,128)(2,1)S(1)}, u32[]{:S(2)}, u32[]{:S(2)}) %collective-permute-start.26) | collective-permute-done | bytes 16416 | tf_op jit(solution)/shard_map/ppermute | solution.py:11
  481.1 3.8 collective-permute-start.27
  484.9 5.8 %collective-permute-done.27 = bf16[8,1,8,128]{3,2,1,0:T(8,128)(2,1)S(1)} collective-permute-done((bf16[8,1,8,128]{3,2,1,0:T(8,128)(2,1)S(1)}, bf16[8,1,8,128]{3,2,1,0:T(8,128)(2,1)S(1)}, u32[]{:S(2)}, u32[]{:S(2)}) %collective-permute-start.27) | collective-permute-done | bytes 16416 | tf_op jit(solution)/shard_map/ppermute | solution.py:11
  490.7 11.6 %all_gather.18 = bf16[16,8,8,128]{3,2,1,0:T(8,128)(2,1)S(1)} all-gather(bf16[16,1,8,128]{3,2,1,0:T(8,128)(2,1)S(1)} %bitcast.198), channel_id=1, replica_groups=mesh['row'=64,'col'=8] {'col'}, dimensions={1}, use_global_device_ids=true | all-gather | bytes 294912 | tf_op jit(solution)/shard_map/all_gather | solution.py:47
  502.8 2.1 collective-permute-start.28
  504.9 4.1 collective-permute-done.28
  511.0 4.9 collective-permute-done.29
  517.2 11.6 %all_gather.19 = bf16[16,8,8,128]{3,2,1,0:T(8,128)(2,1)S(1)} all-gather(bf16[16,1,8,128]{3,2,1,0:T(8,128)(2,1)S(1)} %subtract_convert_fusion), channel_id=1, replica_groups=mesh['row'=64,'col'=8] {'col'}, dimensions={1}, use_global_device_ids=true | all-gather | bytes 294912 | tf_op jit(solution)/shard_map/all_gather | solution.py:47
  529.3 2.1 collective-permute-start.30
  531.5 4.1 collective-permute-done.30
  537.5 4.9 collective-permute-done.31
  (118 shorter events, 48.2 us)
Async XLA Ops:
  7.2 14.5 %copy-start = (bf16[1024,512]{1,0:T(8,128)(2,1)S(1)}, bf16[1024,512]{1,0:T(8,128)(2,1)}, u32[]{:S(2)}) copy-start(bf16[1024,512]{1,0:T(8,128)(2,1)} %param.10) | copy-start | bytes 3145732
  7.2 132.9 %all-reduce.11.cloned.1.call-start = ((), (), s32[]{:S(2)}) async-start(), calls=%async_computation | async-start | bytes 1048576
  7.2 6.2 %collective-permute-start = (bf16[16,1,8,128]{3,2,1,0:T(8,128)(2,1)}, bf16[16,1,8,128]{3,2,1,0:T(8,128)(2,1)S(1)}, u32[]{:S(2)}, u32[]{:S(2)}) collective-permute-start(bf16[16,1,8,128]{3,2,1,0:T(8,128)(2,1)} %bitcast.202), channel_id=1, source_target_pairs={{0,8},{8,0},{16,24},{24,16},{32,40},{40,32},{48,56},{56,48},{64,72... | collective-permute-start | bytes 98312 | tf_op jit(solution)/shard_map/ppermute | solution.py:11
  9.7 3.6 copy-start.5
  13.4 8.3 %collective-permute-start.1 = (bf16[16,2,8,128]{3,2,1,0:T(8,128)(2,1)S(1)}, bf16[16,2,8,128]{3,2,1,0:T(8,128)(2,1)S(1)}, u32[]{:S(2)}, u32[]{:S(2)}) collective-permute-start(bf16[16,2,8,128]{3,2,1,0:T(8,128)(2,1)S(1)} %maximum_select_fusion.5), channel_id=1, source_target_pairs={{0,16},{8,24},{16,0},{24,8},{32,48},{40,56},{48,32},{56,40},{64,80... | collective-permute-start | bytes 196616 | tf_op jit(solution)/shard_map/ppermute | solution.py:11
  51.5 4.9 copy-start.3
  52.2 6.3 %collective-permute-start.2 = (bf16[16,1,8,128]{3,2,1,0:T(8,128)(2,1)S(1)}, bf16[16,1,8,128]{3,2,1,0:T(8,128)(2,1)S(1)}, u32[]{:S(2)}, u32[]{:S(2)}) collective-permute-start(bf16[16,1,8,128]{3,2,1,0:T(8,128)(2,1)S(1)} %dynamic-slice_convert_fusion.5), channel_id=1, source_target_pairs={{0,8},{8,0},{16,24},{24,16},{32,40},{40,32},{48,56},{56,48},{64,72... | collective-permute-start | bytes 98312 | tf_op jit(solution)/shard_map/ppermute | solution.py:11
  58.5 7.1 %collective-permute-start.3 = (bf16[16,2,8,128]{3,2,1,0:T(8,128)(2,1)S(1)}, bf16[16,2,8,128]{3,2,1,0:T(8,128)(2,1)S(1)}, u32[]{:S(2)}, u32[]{:S(2)}) collective-permute-start(bf16[16,2,8,128]{3,2,1,0:T(8,128)(2,1)S(1)} %maximum_select_fusion.6), channel_id=1, source_target_pairs={{0,16},{8,24},{16,0},{24,8},{32,48},{40,56},{48,32},{56,40},{64,80... | collective-permute-start | bytes 196616 | tf_op jit(solution)/shard_map/ppermute | solution.py:11
  66.8 106.7 %copy-start.1 = (bf16[512,512]{1,0:T(8,128)(2,1)S(1)}, bf16[512,512]{1,0:T(8,128)(2,1)}, u32[]{:S(2)}) copy-start(bf16[512,512]{1,0:T(8,128)(2,1)} %param.11) | copy-start | bytes 1572868
  66.9 230.8 %all-reduce.13.cloned.1.call-start = ((), (), s32[]{:S(2)}) async-start(), calls=%async_computation.1 | async-start | bytes 524288
  141.5 9.6 %copy-start.6 = (bf16[64,128]{1,0:T(8,128)(2,1)S(1)}, bf16[64,128]{1,0:T(8,128)(2,1)}, u32[]{:S(2)}) copy-start(bf16[64,128]{1,0:T(8,128)(2,1)} %param.16) | copy-start | bytes 49156
  141.6 9.5 %collective-permute-start.4 = (bf16[8,1,8,128]{3,2,1,0:T(8,128)(2,1)S(1)}, bf16[8,1,8,128]{3,2,1,0:T(8,128)(2,1)S(1)}, u32[]{:S(2)}, u32[]{:S(2)}) collective-permute-start(bf16[8,1,8,128]{3,2,1,0:T(8,128)(2,1)S(1)} %dynamic-slice_convert_fusion.13), channel_id=1, source_target_pairs={{0,32},{8,40},{16,48},{24,56},{32,0},{40,8},{48,16},{56,24},{64,96... | collective-permute-start | bytes 49160 | tf_op jit(solution)/shard_map/ppermute | solution.py:11
  151.1 5.6 %collective-permute-start.5 = (bf16[8,1,8,128]{3,2,1,0:T(8,128)(2,1)S(1)}, bf16[8,1,8,128]{3,2,1,0:T(8,128)(2,1)S(1)}, u32[]{:S(2)}, u32[]{:S(2)}) collective-permute-start(bf16[8,1,8,128]{3,2,1,0:T(8,128)(2,1)S(1)} %fusion.8), channel_id=1, source_target_pairs={{0,8},{8,0},{16,24},{24,16},{32,40},{40,32},{48,56},{56,48},{64,72... | collective-permute-start | bytes 49160 | tf_op jit(solution)/shard_map/ppermute | solution.py:11
  156.8 6.7 %collective-permute-start.6 = (bf16[8,2,8,128]{3,2,1,0:T(8,128)(2,1)S(1)}, bf16[8,2,8,128]{3,2,1,0:T(8,128)(2,1)S(1)}, u32[]{:S(2)}, u32[]{:S(2)}) collective-permute-start(bf16[8,2,8,128]{3,2,1,0:T(8,128)(2,1)S(1)} %maximum_select_fusion.10), channel_id=1, source_target_pairs={{0,16},{8,24},{16,0},{24,8},{32,48},{40,56},{48,32},{56,40},{64,80... | collective-permute-start | bytes 98312 | tf_op jit(solution)/shard_map/ppermute | solution.py:11
  163.5 10.1 %collective-permute-start.7 = (bf16[8,4,8,128]{3,2,1,0:T(8,128)(2,1)S(1)}, bf16[8,4,8,128]{3,2,1,0:T(8,128)(2,1)S(1)}, u32[]{:S(2)}, u32[]{:S(2)}) collective-permute-start(bf16[8,4,8,128]{3,2,1,0:T(8,128)(2,1)S(1)} %maximum_select_fusion.7), channel_id=1, source_target_pairs={{0,32},{8,40},{16,48},{24,56},{32,0},{40,8},{48,16},{56,24},{64,96... | collective-permute-start | bytes 196616 | tf_op jit(solution)/shard_map/ppermute | solution.py:11
  200.3 8.9 %copy-start.4 = (bf16[8,8,8,128]{3,2,1,0:T(8,128)(2,1)}, bf16[8,8,8,128]{3,2,1,0:T(8,128)(2,1)S(1)}, u32[]{:S(2)}) copy-start(bf16[8,8,8,128]{3,2,1,0:T(8,128)(2,1)S(1)} %all-reduce.15) | copy-start | bytes 393220
  201.0 5.6 %collective-permute-start.8 = (bf16[8,1,8,128]{3,2,1,0:T(8,128)(2,1)S(1)}, bf16[8,1,8,128]{3,2,1,0:T(8,128)(2,1)S(1)}, u32[]{:S(2)}, u32[]{:S(2)}) collective-permute-start(bf16[8,1,8,128]{3,2,1,0:T(8,128)(2,1)S(1)} %dynamic-slice_convert_fusion.9), channel_id=1, source_target_pairs={{0,8},{8,0},{16,24},{24,16},{32,40},{40,32},{48,56},{56,48},{64,72... | collective-permute-start | bytes 49160 | tf_op jit(solution)/shard_map/ppermute | solution.py:11
  206.6 6.7 %collective-permute-start.9 = (bf16[8,2,8,128]{3,2,1,0:T(8,128)(2,1)S(1)}, bf16[8,2,8,128]{3,2,1,0:T(8,128)(2,1)S(1)}, u32[]{:S(2)}, u32[]{:S(2)}) collective-permute-start(bf16[8,2,8,128]{3,2,1,0:T(8,128)(2,1)S(1)} %maximum_select_fusion.11), channel_id=1, source_target_pairs={{0,16},{8,24},{16,0},{24,8},{32,48},{40,56},{48,32},{56,40},{64,80... | collective-permute-start | bytes 98312 | tf_op jit(solution)/shard_map/ppermute | solution.py:11
  213.3 10.1 %collective-permute-start.10 = (bf16[8,4,8,128]{3,2,1,0:T(8,128)(2,1)S(1)}, bf16[8,4,8,128]{3,2,1,0:T(8,128)(2,1)S(1)}, u32[]{:S(2)}, u32[]{:S(2)}) collective-permute-start(bf16[8,4,8,128]{3,2,1,0:T(8,128)(2,1)S(1)} %maximum_select_fusion.8), channel_id=1, source_target_pairs={{0,32},{8,40},{16,48},{24,56},{32,0},{40,8},{48,16},{56,24},{64,96... | collective-permute-start | bytes 196616 | tf_op jit(solution)/shard_map/ppermute | solution.py:11
  299.0 5.7 %copy-start.7 = (bf16[32,128]{1,0:T(8,128)(2,1)S(1)}, bf16[32,128]{1,0:T(8,128)(2,1)}, u32[]{:S(2)}) copy-start(bf16[32,128]{1,0:T(8,128)(2,1)} %param.17) | copy-start | bytes 24580
  299.0 5.7 %collective-permute-start.11 = (bf16[4,1,8,128]{3,2,1,0:T(8,128)(2,1)S(1)}, bf16[4,1,8,128]{3,2,1,0:T(8,128)(2,1)S(1)}, u32[]{:S(2)}, u32[]{:S(2)}) collective-permute-start(bf16[4,1,8,128]{3,2,1,0:T(8,128)(2,1)S(1)} %dynamic-slice_convert_fusion.16), channel_id=1, source_target_pairs={{0,64},{8,72},{16,80},{24,88},{32,96},{40,104},{48,112},{56,120},{... | collective-permute-start | bytes 24584 | tf_op jit(solution)/shard_map/ppermute | solution.py:11
  304.7 28.3 %copy-start.2 = (bf16[256,512]{1,0:T(8,128)(2,1)S(1)}, bf16[256,512]{1,0:T(8,128)(2,1)}, u32[]{:S(2)}) copy-start(bf16[256,512]{1,0:T(8,128)(2,1)} %param.12) | copy-start | bytes 786436
  304.7 5.7 %collective-permute-start.12 = (bf16[4,1,8,128]{3,2,1,0:T(8,128)(2,1)S(1)}, bf16[4,1,8,128]{3,2,1,0:T(8,128)(2,1)S(1)}, u32[]{:S(2)}, u32[]{:S(2)}) collective-permute-start(bf16[4,1,8,128]{3,2,1,0:T(8,128)(2,1)S(1)} %fusion.12), channel_id=1, source_target_pairs={{0,8},{8,0},{16,24},{24,16},{32,40},{40,32},{48,56},{56,48},{64,72... | collective-permute-start | bytes 24584 | tf_op jit(solution)/shard_map/ppermute | solution.py:11
  310.4 6.7 %collective-permute-start.13 = (bf16[4,2,8,128]{3,2,1,0:T(8,128)(2,1)S(1)}, bf16[4,2,8,128]{3,2,1,0:T(8,128)(2,1)S(1)}, u32[]{:S(2)}, u32[]{:S(2)}) collective-permute-start(bf16[4,2,8,128]{3,2,1,0:T(8,128)(2,1)S(1)} %maximum_select_fusion.14), channel_id=1, source_target_pairs={{0,16},{8,24},{16,0},{24,8},{32,48},{40,56},{48,32},{56,40},{64,80... | collective-permute-start | bytes 49160 | tf_op jit(solution)/shard_map/ppermute | solution.py:11
  317.1 9.7 %collective-permute-start.14 = (bf16[4,4,8,128]{3,2,1,0:T(8,128)(2,1)S(1)}, bf16[4,4,8,128]{3,2,1,0:T(8,128)(2,1)S(1)}, u32[]{:S(2)}, u32[]{:S(2)}) collective-permute-start(bf16[4,4,8,128]{3,2,1,0:T(8,128)(2,1)S(1)} %maximum_select_fusion.12), channel_id=1, source_target_pairs={{0,32},{8,40},{16,48},{24,56},{32,0},{40,8},{48,16},{56,24},{64,96... | collective-permute-start | bytes 98312 | tf_op jit(solution)/shard_map/ppermute | solution.py:11
  326.8 6.2 %collective-permute-start.15 = (bf16[4,8,8,128]{3,2,1,0:T(8,128)(2,1)S(1)}, bf16[4,8,8,128]{3,2,1,0:T(8,128)(2,1)S(1)}, u32[]{:S(2)}, u32[]{:S(2)}) collective-permute-start(bf16[4,8,8,128]{3,2,1,0:T(8,128)(2,1)S(1)} %maximum_select_fusion.9), channel_id=1, source_target_pairs={{0,64},{8,72},{16,80},{24,88},{32,96},{40,104},{48,112},{56,120},{... | collective-permute-start | bytes 196616 | tf_op jit(solution)/shard_map/ppermute | solution.py:11
  374.7 6.3 %collective-permute-start.16 = (bf16[4,8,8,128]{3,2,1,0:T(8,128)(2,1)S(1)}, bf16[4,8,8,128]{3,2,1,0:T(8,128)(2,1)}, u32[]{:S(2)}, u32[]{:S(2)}) collective-permute-start(bf16[4,8,8,128]{3,2,1,0:T(8,128)(2,1)S(1)} %fusion), channel_id=1, source_target_pairs={{0,8},{8,0},{16,24},{24,16},{32,40},{40,32},{48,56},{56,48},{64,72... | collective-permute-start | bytes 196616 | tf_op jit(solution)/shard_map/ppermute | solution.py:11
  381.9 7.1 %collective-permute-start.17 = (bf16[4,4,8,128]{3,2,1,0:T(8,128)(2,1)S(1)}, bf16[4,4,8,128]{3,2,1,0:T(8,128)(2,1)S(1)}, u32[]{:S(2)}, u32[]{:S(2)}) collective-permute-start(bf16[4,4,8,128]{3,2,1,0:T(8,128)(2,1)S(1)} %fusion.6), channel_id=1, source_target_pairs={{0,16},{8,24},{16,0},{24,8},{32,48},{40,56},{48,32},{56,40},{64,80... | collective-permute-start | bytes 98312 | tf_op jit(solution)/shard_map/ppermute | solution.py:11
  389.0 9.5 %collective-permute-start.18 = (bf16[4,2,8,128]{3,2,1,0:T(8,128)(2,1)S(1)}, bf16[4,2,8,128]{3,2,1,0:T(8,128)(2,1)S(1)}, u32[]{:S(2)}, u32[]{:S(2)}) collective-permute-start(bf16[4,2,8,128]{3,2,1,0:T(8,128)(2,1)S(1)} %fusion.11), channel_id=1, source_target_pairs={{0,32},{8,40},{16,48},{24,56},{32,0},{40,8},{48,16},{56,24},{64,96... | collective-permute-start | bytes 49160 | tf_op jit(solution)/shard_map/ppermute | solution.py:11
  398.6 5.5 %collective-permute-start.19 = (bf16[4,1,8,128]{3,2,1,0:T(8,128)(2,1)S(1)}, bf16[4,1,8,128]{3,2,1,0:T(8,128)(2,1)S(1)}, u32[]{:S(2)}, u32[]{:S(2)}) collective-permute-start(bf16[4,1,8,128]{3,2,1,0:T(8,128)(2,1)S(1)} %dynamic-slice_convert_fusion.15), channel_id=1, source_target_pairs={{0,64},{8,72},{16,80},{24,88},{32,96},{40,104},{48,112},{56,120},{... | collective-permute-start | bytes 24584 | tf_op jit(solution)/shard_map/ppermute | solution.py:11
  404.7 5.5 %collective-permute-start.20 = (bf16[4,1,8,128]{3,2,1,0:T(8,128)(2,1)S(1)}, bf16[4,1,8,128]{3,2,1,0:T(8,128)(2,1)S(1)}, u32[]{:S(2)}, u32[]{:S(2)}) collective-permute-start(bf16[4,1,8,128]{3,2,1,0:T(8,128)(2,1)S(1)} %get-tuple-element.6), channel_id=1, source_target_pairs={{0,64},{8,72},{16,80},{24,88},{32,96},{40,104},{48,112},{56,120},{... | collective-permute-start | bytes 24584 | tf_op jit(solution)/shard_map/ppermute | solution.py:11
  421.9 6.2 %collective-permute-start.21 = (bf16[8,4,8,128]{3,2,1,0:T(8,128)(2,1)S(1)}, bf16[8,4,8,128]{3,2,1,0:T(8,128)(2,1)S(1)}, u32[]{:S(2)}, u32[]{:S(2)}) collective-permute-start(bf16[8,4,8,128]{3,2,1,0:T(8,128)(2,1)S(1)} %fusion.1), channel_id=1, source_target_pairs={{0,8},{8,0},{16,24},{24,16},{32,40},{40,32},{48,56},{56,48},{64,72... | collective-permute-start | bytes 196616 | tf_op jit(solution)/shard_map/ppermute | solution.py:11
  428.2 7.0 %collective-permute-start.22 = (bf16[8,2,8,128]{3,2,1,0:T(8,128)(2,1)S(1)}, bf16[8,2,8,128]{3,2,1,0:T(8,128)(2,1)S(1)}, u32[]{:S(2)}, u32[]{:S(2)}) collective-permute-start(bf16[8,2,8,128]{3,2,1,0:T(8,128)(2,1)S(1)} %fusion.7), channel_id=1, source_target_pairs={{0,16},{8,24},{16,0},{24,8},{32,48},{40,56},{48,32},{56,40},{64,80... | collective-permute-start | bytes 98312 | tf_op jit(solution)/shard_map/ppermute | solution.py:11
  435.3 9.5 %collective-permute-start.23 = (bf16[8,1,8,128]{3,2,1,0:T(8,128)(2,1)S(1)}, bf16[8,1,8,128]{3,2,1,0:T(8,128)(2,1)S(1)}, u32[]{:S(2)}, u32[]{:S(2)}) collective-permute-start(bf16[8,1,8,128]{3,2,1,0:T(8,128)(2,1)S(1)} %dynamic-slice_convert_fusion.11), channel_id=1, source_target_pairs={{0,32},{8,40},{16,48},{24,56},{32,0},{40,8},{48,16},{56,24},{64,96... | collective-permute-start | bytes 49160 | tf_op jit(solution)/shard_map/ppermute | solution.py:11
  457.9 6.2 %collective-permute-start.24 = (bf16[8,4,8,128]{3,2,1,0:T(8,128)(2,1)S(1)}, bf16[8,4,8,128]{3,2,1,0:T(8,128)(2,1)S(1)}, u32[]{:S(2)}, u32[]{:S(2)}) collective-permute-start(bf16[8,4,8,128]{3,2,1,0:T(8,128)(2,1)S(1)} %fusion.2), channel_id=1, source_target_pairs={{0,8},{8,0},{16,24},{24,16},{32,40},{40,32},{48,56},{56,48},{64,72... | collective-permute-start | bytes 196616 | tf_op jit(solution)/shard_map/ppermute | solution.py:11
  464.2 6.8 %collective-permute-start.25 = (bf16[8,2,8,128]{3,2,1,0:T(8,128)(2,1)S(1)}, bf16[8,2,8,128]{3,2,1,0:T(8,128)(2,1)S(1)}, u32[]{:S(2)}, u32[]{:S(2)}) collective-permute-start(bf16[8,2,8,128]{3,2,1,0:T(8,128)(2,1)S(1)} %fusion.5), channel_id=1, source_target_pairs={{0,16},{8,24},{16,0},{24,8},{32,48},{40,56},{48,32},{56,40},{64,80... | collective-permute-start | bytes 98312 | tf_op jit(solution)/shard_map/ppermute | solution.py:11
  471.0 9.5 %collective-permute-start.26 = (bf16[8,1,8,128]{3,2,1,0:T(8,128)(2,1)S(1)}, bf16[8,1,8,128]{3,2,1,0:T(8,128)(2,1)S(1)}, u32[]{:S(2)}, u32[]{:S(2)}) collective-permute-start(bf16[8,1,8,128]{3,2,1,0:T(8,128)(2,1)S(1)} %dynamic-slice_convert_fusion.10), channel_id=1, source_target_pairs={{0,32},{8,40},{16,48},{24,56},{32,0},{40,8},{48,16},{56,24},{64,96... | collective-permute-start | bytes 49160 | tf_op jit(solution)/shard_map/ppermute | solution.py:11
  481.1 9.5 %collective-permute-start.27 = (bf16[8,1,8,128]{3,2,1,0:T(8,128)(2,1)S(1)}, bf16[8,1,8,128]{3,2,1,0:T(8,128)(2,1)S(1)}, u32[]{:S(2)}, u32[]{:S(2)}) collective-permute-start(bf16[8,1,8,128]{3,2,1,0:T(8,128)(2,1)S(1)} %get-tuple-element.4), channel_id=1, source_target_pairs={{0,32},{8,40},{16,48},{24,56},{32,0},{40,8},{48,16},{56,24},{64,96... | collective-permute-start | bytes 49160 | tf_op jit(solution)/shard_map/ppermute | solution.py:11
  502.8 6.2 %collective-permute-start.28 = (bf16[16,2,8,128]{3,2,1,0:T(8,128)(2,1)S(1)}, bf16[16,2,8,128]{3,2,1,0:T(8,128)(2,1)S(1)}, u32[]{:S(2)}, u32[]{:S(2)}) collective-permute-start(bf16[16,2,8,128]{3,2,1,0:T(8,128)(2,1)S(1)} %fusion.3), channel_id=1, source_target_pairs={{0,8},{8,0},{16,24},{24,16},{32,40},{40,32},{48,56},{56,48},{64,72... | collective-permute-start | bytes 196616 | tf_op jit(solution)/shard_map/ppermute | solution.py:11
  509.0 6.8 %collective-permute-start.29 = (bf16[16,1,8,128]{3,2,1,0:T(8,128)(2,1)S(1)}, bf16[16,1,8,128]{3,2,1,0:T(8,128)(2,1)S(1)}, u32[]{:S(2)}, u32[]{:S(2)}) collective-permute-start(bf16[16,1,8,128]{3,2,1,0:T(8,128)(2,1)S(1)} %dynamic-slice_convert_fusion.7), channel_id=1, source_target_pairs={{0,16},{8,24},{16,0},{24,8},{32,48},{40,56},{48,32},{56,40},{64,80... | collective-permute-start | bytes 98312 | tf_op jit(solution)/shard_map/ppermute | solution.py:11
  529.3 6.2 %collective-permute-start.30 = (bf16[16,2,8,128]{3,2,1,0:T(8,128)(2,1)S(1)}, bf16[16,2,8,128]{3,2,1,0:T(8,128)(2,1)S(1)}, u32[]{:S(2)}, u32[]{:S(2)}) collective-permute-start(bf16[16,2,8,128]{3,2,1,0:T(8,128)(2,1)S(1)} %fusion.4), channel_id=1, source_target_pairs={{0,8},{8,0},{16,24},{24,16},{32,40},{40,32},{48,56},{56,48},{64,72... | collective-permute-start | bytes 196616 | tf_op jit(solution)/shard_map/ppermute | solution.py:11
  535.6 6.8 %collective-permute-start.31 = (bf16[16,1,8,128]{3,2,1,0:T(8,128)(2,1)S(1)}, bf16[16,1,8,128]{3,2,1,0:T(8,128)(2,1)S(1)}, u32[]{:S(2)}, u32[]{:S(2)}) collective-permute-start(bf16[16,1,8,128]{3,2,1,0:T(8,128)(2,1)S(1)} %dynamic-slice_convert_fusion.6), channel_id=1, source_target_pairs={{0,16},{8,24},{16,0},{24,8},{32,48},{40,56},{48,32},{56,40},{64,80... | collective-permute-start | bytes 98312 | tf_op jit(solution)/shard_map/ppermute | solution.py:11
Sparse Core Ops, SparseCore 0:
  67.0 73.0 all-reduce.10
  225.6 71.9 all-reduce.12
where the time goes:
time: 552 us; the launch traced here: 550 us
  waiting for transfers between devices  261 us (47%)
  blocking collectives  138 us (25%)
  starting transfers between devices  104 us (19%)
  local copies, waits for them, and re-layouts  17.1 us (3%)
  between operations  14.9 us (3%)
  other arithmetic  7.5 us (1%)
  matrix products  7.2 us (1%)
    unnamed x4, waiting for transfers between devices  145 us
    ppermute x32, waiting for transfers between devices, partner(): lax.ppermute(value, axis, [(i, i ^ 1 << stride) for i in range(lax.axis_s...  116 us
    ppermute x32, starting transfers between devices, partner(): lax.ppermute(value, axis, [(i, i ^ 1 << stride) for i in range(lax.axis_s...  104 us
    unnamed x3, blocking collectives  80.7 us
    all_gather x5, blocking collectives, column_join(): gathered = lax.all_gather(pieces, 'col', axis=1, tiled=True)  57 us
  transfers between devices with their start and end apart: 34, of which 33 were waited for; matrix products, arithmetic and copies ran while one was open for 2% of the time, Pallas kernels for 0%

commit v1 on v0

--- a/solution.py
+++ b/solution.py
@@ -44,7 +44,9 @@
 
 
 def column_join(pieces):
-    gathered = lax.all_gather(pieces, "col", axis=1, tiled=True)
+    gathered = jnp.concatenate(
+        lax.all_to_all(jnp.stack([pieces] * lax.axis_size("col")), "col", 0, 0), axis=1
+    )
     return gathered.reshape(-1, gathered.shape[-1])
 
 

time: 552 us -> 541 us (0.980)
  blocking collectives: 138 us -> 118 us
  waiting for transfers between devices: 261 us -> 267 us
    all_gather x5 -> x0, blocking collectives: 57 us -> none  [column_join(): gathered = lax.all_gather(pieces, 'col', axis=1, tiled=True)]
    all_to_all x0 -> x4, blocking collectives: none -> 36.8 us  [column_join(): lax.all_to_all(jnp.stack([pieces] * lax.axis_size('col')), 'col', 0, 0)]
    all_to_all x0 -> x1, waiting for transfers between devices: none -> 5.54 us  [column_join(): lax.all_to_all(jnp.stack([pieces] * lax.axis_size('col')), 'col', 0, 0)]
  transfers between devices with their start and end apart: 34 -> 35, of which waited for: 33 -> 34; matrix products, arithmetic and copies ran while one was open for 2% -> 2% of each run, Pallas kernels for 0% -> 0%
where the time goes in v1:
time: 541 us; the launch traced here: 539 us
  waiting for transfers between devices  267 us (49%)
  blocking collectives  118 us (22%)
  starting transfers between devices  107 us (20%)
  local copies, waits for them, and re-layouts  17.6 us (3%)
  between operations  14.9 us (3%)
  other arithmetic  7.5 us (1%)
  matrix products  7.24 us (1%)
    unnamed x4, waiting for transfers between devices  145 us
    ppermute x32, waiting for transfers between devices, partner(): lax.ppermute(value, axis, [(i, i ^ 1 << stride) for i in range(lax.axis_s...  116 us
    ppermute x32, starting transfers between devices, partner(): lax.ppermute(value, axis, [(i, i ^ 1 << stride) for i in range(lax.axis_s...  104 us
    unnamed x3, blocking collectives  80.8 us
    all_to_all x4, blocking collectives, column_join(): lax.all_to_all(jnp.stack([pieces] * lax.axis_size('col')), 'col', 0, 0)  36.8 us
  transfers between devices with their start and end apart: 35, of which 34 were waited for; matrix products, arithmetic and copies ran while one was open for 2% of the time, Pallas kernels for 0%

profile of v1, /device:TPU:24, one launch (start us, length us, event | category | flops | bytes accessed | tf_op | source)
XLA Modules:
  0.0 539.1 jit_solution(15964203903044045142)
XLA Ops:
  7.2 2.5 collective-permute-start
  13.4 6.0 %collective-permute-start.1 = (bf16[16,2,8,128]{3,2,1,0:T(8,128)(2,1)S(1)}, bf16[16,2,8,128]{3,2,1,0:T(8,128)(2,1)S(1)}, u32[]{:S(2)}, u32[]{:S(2)}) collective-permute-start(bf16[16,2,8,128]{3,2,1,0:T(8,128)(2,1)S(1)} %maximum_select_fusion.5), channel_id=1, source_target_pairs={{0,16},{8,24},{16,0},{24,8},{32,48},{40,56},{48,32},{56,40},{64,80... | collective-permute-start | bytes 196616 | tf_op jit(solution)/shard_map/ppermute | solution.py:11
  19.4 2.2 collective-permute-done.1
  22.4 29.2 %all-reduce.14 = bf16[16,8,8,128]{3,2,1,0:T(8,128)(2,1)S(1)} all-reduce(f32[16,8,8,128]{3,2,1,0:T(8,128)S(1)} %bitcast.191), channel_id=2, replica_groups=mesh['row'=64,'col'=8] {'col'}, use_global_device_ids=true, to_apply=%region_0.1.clone | all-reduce | flops 131072 | bytes 786432
  52.2 4.1 collective-permute-start.2
  58.5 4.8 collective-permute-start.3
  67.0 73.1 %all-reduce.11.cloned.1.call-done = f32[16,8,8,128]{3,2,1,0:T(8,128)} async-done(((f32[16,8,8,128]{3,2,1,0:T(8,128)}), f32[16,8,8,128]{3,2,1,0:T(8,128)}) %all-reduce.11.cloned.1.call-update) | async-done | bytes 524304
  141.6 4.7 collective-permute-start.4
  146.3 4.9 collective-permute-done.4
  151.2 2.6 collective-permute-start.5
  153.8 3.0 collective-permute-done.5
  156.8 2.4 collective-permute-start.6
  159.3 4.3 collective-permute-done.6
  163.5 4.8 collective-permute-start.7
  169.0 4.6 collective-permute-done.7
  174.1 26.4 %all-reduce.15 = bf16[8,8,8,128]{3,2,1,0:T(8,128)(2,1)S(1)} all-reduce(f32[8,8,8,128]{3,2,1,0:T(8,128)S(1)} %bitcast.192), channel_id=4, replica_groups=mesh['row'=64,'col'=8] {'col'}, use_global_device_ids=true, to_apply=%region_3.4.clone | all-reduce | flops 65536 | bytes 393216
  201.2 3.4 collective-permute-start.8
  204.6 2.2 collective-permute-done.8
  206.8 2.5 collective-permute-start.9
  213.5 5.2 collective-permute-start.10
  220.9 2.7 collective-permute-done.10
  225.7 72.2 %all-reduce.13.cloned.1.call-done = f32[8,8,8,128]{3,2,1,0:T(8,128)} async-done(((f32[8,8,8,128]{3,2,1,0:T(8,128)}), f32[8,8,8,128]{3,2,1,0:T(8,128)}) %all-reduce.13.cloned.1.call-update) | async-done | bytes 262160
  299.3 3.7 collective-permute-start.11
  304.9 2.4 collective-permute-start.12
  307.4 3.1 collective-permute-done.12
  310.5 2.4 collective-permute-start.13
  312.9 4.3 collective-permute-done.13
  317.2 4.5 collective-permute-start.14
  321.7 5.2 collective-permute-done.14
  326.9 3.6 collective-permute-start.15
  330.5 2.6 collective-permute-done.15
  335.0 25.3 %all-reduce.16 = bf16[4,8,8,128]{3,2,1,0:T(8,128)(2,1)} all-reduce(f32[4,8,8,128]{3,2,1,0:T(8,128)S(1)} %bitcast.206), channel_id=6, replica_groups=mesh['row'=64,'col'=8] {'col'}, use_global_device_ids=true, to_apply=%region_6.7.clone | all-reduce | flops 32768 | bytes 196608
  362.3 3.4 all-to-all-start
  365.6 5.5 %all-to-all-done = bf16[8,4,1,8,128]{4,3,1,2,0:T(8,128)(2,1)S(1)} async-done(((bf16[8,4,1,8,128]{4,3,1,2,0:T(8,128)(2,1)}), bf16[8,4,1,8,128]{4,3,1,2,0:T(8,128)(2,1)S(1)}, u32[]{:S(2)}, u32[]{:S(2)}) %all-to-all-start) | async-done | bytes 65568 | tf_op jit(solution)/shard_map/all_to_all | solution.py:48
  373.2 2.7 collective-permute-start.16
  375.9 3.6 collective-permute-done.16
  380.3 2.2 collective-permute-start.17
  382.6 4.8 collective-permute-done.17
  387.4 4.2 collective-permute-start.18
  391.6 5.4 collective-permute-done.18
  397.0 3.6 collective-permute-start.19
  403.1 3.5 collective-permute-start.20
  408.7 8.5 %all_to_all.25 = bf16[8,8,1,8,128]{4,3,1,2,0:T(8,128)(2,1)S(1)} all-to-all(bf16[8,8,1,8,128]{4,3,1,2,0:T(8,128)(2,1)S(1)} %stack.11), channel_id=1, replica_groups=mesh['row'=64,'col'=8] {'col'}, dimensions={0} | all-to-all | bytes 262144 | tf_op jit(solution)/shard_map/all_to_all | solution.py:48
  417.6 2.4 collective-permute-start.21
  420.0 3.7 collective-permute-done.21
  425.7 5.1 collective-permute-done.22
  430.8 3.9 collective-permute-start.23
  434.7 5.7 %collective-permute-done.23 = bf16[8,1,8,128]{3,2,1,0:T(8,128)(2,1)S(1)} collective-permute-done((bf16[8,1,8,128]{3,2,1,0:T(8,128)(2,1)S(1)}, bf16[8,1,8,128]{3,2,1,0:T(8,128)(2,1)S(1)}, u32[]{:S(2)}, u32[]{:S(2)}) %collective-permute-start.23) | collective-permute-done | bytes 16416 | tf_op jit(solution)/shard_map/ppermute | solution.py:11
  441.7 8.5 %all_to_all.26 = bf16[8,8,1,8,128]{4,3,1,2,0:T(8,128)(2,1)S(1)} all-to-all(bf16[8,8,1,8,128]{4,3,1,2,0:T(8,128)(2,1)S(1)} %stack.12), channel_id=1, replica_groups=mesh['row'=64,'col'=8] {'col'}, dimensions={0} | all-to-all | bytes 262144 | tf_op jit(solution)/shard_map/all_to_all | solution.py:48
  450.7 2.1 collective-permute-start.24
  452.8 4.0 collective-permute-done.24
  458.8 4.8 collective-permute-done.25
  463.6 3.8 collective-permute-start.26
  467.5 5.7 %collective-permute-done.26 = bf16[8,1,8,128]{3,2,1,0:T(8,128)(2,1)S(1)} collective-permute-done((bf16[8,1,8,128]{3,2,1,0:T(8,128)(2,1)S(1)}, bf16[8,1,8,128]{3,2,1,0:T(8,128)(2,1)S(1)}, u32[]{:S(2)}, u32[]{:S(2)}) %collective-permute-start.26) | collective-permute-done | bytes 16416 | tf_op jit(solution)/shard_map/ppermute | solution.py:11
  473.8 3.8 collective-permute-start.27
  477.6 5.7 %collective-permute-done.27 = bf16[8,1,8,128]{3,2,1,0:T(8,128)(2,1)S(1)} collective-permute-done((bf16[8,1,8,128]{3,2,1,0:T(8,128)(2,1)S(1)}, bf16[8,1,8,128]{3,2,1,0:T(8,128)(2,1)S(1)}, u32[]{:S(2)}, u32[]{:S(2)}) %collective-permute-start.27) | collective-permute-done | bytes 16416 | tf_op jit(solution)/shard_map/ppermute | solution.py:11
  483.4 9.9 %all_to_all.27 = bf16[8,16,1,8,128]{4,3,1,2,0:T(8,128)(2,1)S(1)} all-to-all(bf16[8,16,1,8,128]{4,3,1,2,0:T(8,128)(2,1)S(1)} %stack.13), channel_id=1, replica_groups=mesh['row'=64,'col'=8] {'col'}, dimensions={0} | all-to-all | bytes 524288 | tf_op jit(solution)/shard_map/all_to_all | solution.py:48
  493.8 2.1 collective-permute-start.28
  496.0 4.0 collective-permute-done.28
  502.0 4.8 collective-permute-done.29
  508.2 9.9 %all_to_all.28 = bf16[8,16,1,8,128]{4,3,1,2,0:T(8,128)(2,1)S(1)} all-to-all(bf16[8,16,1,8,128]{4,3,1,2,0:T(8,128)(2,1)S(1)} %stack.14), channel_id=1, replica_groups=mesh['row'=64,'col'=8] {'col'}, dimensions={0} | all-to-all | bytes 524288 | tf_op jit(solution)/shard_map/all_to_all | solution.py:48
  518.7 2.1 collective-permute-start.30
  520.8 4.0 collective-permute-done.30
  526.8 4.8 collective-permute-done.31
  (133 shorter events, 51.2 us)
Async XLA Ops:
  7.2 14.5 %copy-start = (bf16[1024,512]{1,0:T(8,128)(2,1)S(1)}, bf16[1024,512]{1,0:T(8,128)(2,1)}, u32[]{:S(2)}) copy-start(bf16[1024,512]{1,0:T(8,128)(2,1)} %param.10) | copy-start | bytes 3145732
  7.2 132.9 %all-reduce.11.cloned.1.call-start = ((), (), s32[]{:S(2)}) async-start(), calls=%async_computation.5 | async-start | bytes 1048576
  7.2 6.2 %collective-permute-start = (bf16[16,1,8,128]{3,2,1,0:T(8,128)(2,1)}, bf16[16,1,8,128]{3,2,1,0:T(8,128)(2,1)S(1)}, u32[]{:S(2)}, u32[]{:S(2)}) collective-permute-start(bf16[16,1,8,128]{3,2,1,0:T(8,128)(2,1)} %bitcast.226), channel_id=1, source_target_pairs={{0,8},{8,0},{16,24},{24,16},{32,40},{40,32},{48,56},{56,48},{64,72... | collective-permute-start | bytes 98312 | tf_op jit(solution)/shard_map/ppermute | solution.py:11
  9.7 3.6 copy-start.7
  13.4 8.3 %collective-permute-start.1 = (bf16[16,2,8,128]{3,2,1,0:T(8,128)(2,1)S(1)}, bf16[16,2,8,128]{3,2,1,0:T(8,128)(2,1)S(1)}, u32[]{:S(2)}, u32[]{:S(2)}) collective-permute-start(bf16[16,2,8,128]{3,2,1,0:T(8,128)(2,1)S(1)} %maximum_select_fusion.5), channel_id=1, source_target_pairs={{0,16},{8,24},{16,0},{24,8},{32,48},{40,56},{48,32},{56,40},{64,80... | collective-permute-start | bytes 196616 | tf_op jit(solution)/shard_map/ppermute | solution.py:11
  51.5 7.0 %copy-start.4 = (bf16[16,8,8,128]{3,2,1,0:T(8,128)(2,1)}, bf16[16,8,8,128]{3,2,1,0:T(8,128)(2,1)S(1)}, u32[]{:S(2)}) copy-start(bf16[16,8,8,128]{3,2,1,0:T(8,128)(2,1)S(1)} %all-reduce.14) | copy-start | bytes 786436
  52.2 6.3 %collective-permute-start.2 = (bf16[16,1,8,128]{3,2,1,0:T(8,128)(2,1)S(1)}, bf16[16,1,8,128]{3,2,1,0:T(8,128)(2,1)S(1)}, u32[]{:S(2)}, u32[]{:S(2)}) collective-permute-start(bf16[16,1,8,128]{3,2,1,0:T(8,128)(2,1)S(1)} %dynamic-slice_convert_fusion.5), channel_id=1, source_target_pairs={{0,8},{8,0},{16,24},{24,16},{32,40},{40,32},{48,56},{56,48},{64,72... | collective-permute-start | bytes 98312 | tf_op jit(solution)/shard_map/ppermute | solution.py:11
  58.5 7.1 %collective-permute-start.3 = (bf16[16,2,8,128]{3,2,1,0:T(8,128)(2,1)S(1)}, bf16[16,2,8,128]{3,2,1,0:T(8,128)(2,1)S(1)}, u32[]{:S(2)}, u32[]{:S(2)}) collective-permute-start(bf16[16,2,8,128]{3,2,1,0:T(8,128)(2,1)S(1)} %maximum_select_fusion.6), channel_id=1, source_target_pairs={{0,16},{8,24},{16,0},{24,8},{32,48},{40,56},{48,32},{56,40},{64,80... | collective-permute-start | bytes 196616 | tf_op jit(solution)/shard_map/ppermute | solution.py:11
  66.9 106.7 %copy-start.1 = (bf16[512,512]{1,0:T(8,128)(2,1)S(1)}, bf16[512,512]{1,0:T(8,128)(2,1)}, u32[]{:S(2)}) copy-start(bf16[512,512]{1,0:T(8,128)(2,1)} %param.11) | copy-start | bytes 1572868
  66.9 230.9 %all-reduce.13.cloned.1.call-start = ((), (), s32[]{:S(2)}) async-start(), calls=%async_computation.6 | async-start | bytes 524288
  141.6 9.6 %copy-start.8 = (bf16[64,128]{1,0:T(8,128)(2,1)S(1)}, bf16[64,128]{1,0:T(8,128)(2,1)}, u32[]{:S(2)}) copy-start(bf16[64,128]{1,0:T(8,128)(2,1)} %param.16) | copy-start | bytes 49156
  141.6 9.5 %collective-permute-start.4 = (bf16[8,1,8,128]{3,2,1,0:T(8,128)(2,1)S(1)}, bf16[8,1,8,128]{3,2,1,0:T(8,128)(2,1)S(1)}, u32[]{:S(2)}, u32[]{:S(2)}) collective-permute-start(bf16[8,1,8,128]{3,2,1,0:T(8,128)(2,1)S(1)} %dynamic-slice_convert_fusion.12), channel_id=1, source_target_pairs={{0,32},{8,40},{16,48},{24,56},{32,0},{40,8},{48,16},{56,24},{64,96... | collective-permute-start | bytes 49160 | tf_op jit(solution)/shard_map/ppermute | solution.py:11
  151.2 5.6 %collective-permute-start.5 = (bf16[8,1,8,128]{3,2,1,0:T(8,128)(2,1)S(1)}, bf16[8,1,8,128]{3,2,1,0:T(8,128)(2,1)S(1)}, u32[]{:S(2)}, u32[]{:S(2)}) collective-permute-start(bf16[8,1,8,128]{3,2,1,0:T(8,128)(2,1)S(1)} %fusion.9), channel_id=1, source_target_pairs={{0,8},{8,0},{16,24},{24,16},{32,40},{40,32},{48,56},{56,48},{64,72... | collective-permute-start | bytes 49160 | tf_op jit(solution)/shard_map/ppermute | solution.py:11
  156.8 6.7 %collective-permute-start.6 = (bf16[8,2,8,128]{3,2,1,0:T(8,128)(2,1)S(1)}, bf16[8,2,8,128]{3,2,1,0:T(8,128)(2,1)S(1)}, u32[]{:S(2)}, u32[]{:S(2)}) collective-permute-start(bf16[8,2,8,128]{3,2,1,0:T(8,128)(2,1)S(1)} %maximum_select_fusion.10), channel_id=1, source_target_pairs={{0,16},{8,24},{16,0},{24,8},{32,48},{40,56},{48,32},{56,40},{64,80... | collective-permute-start | bytes 98312 | tf_op jit(solution)/shard_map/ppermute | solution.py:11
  163.5 10.1 %collective-permute-start.7 = (bf16[8,4,8,128]{3,2,1,0:T(8,128)(2,1)S(1)}, bf16[8,4,8,128]{3,2,1,0:T(8,128)(2,1)S(1)}, u32[]{:S(2)}, u32[]{:S(2)}) collective-permute-start(bf16[8,4,8,128]{3,2,1,0:T(8,128)(2,1)S(1)} %maximum_select_fusion.7), channel_id=1, source_target_pairs={{0,32},{8,40},{16,48},{24,56},{32,0},{40,8},{48,16},{56,24},{64,96... | collective-permute-start | bytes 196616 | tf_op jit(solution)/shard_map/ppermute | solution.py:11
  174.1 36.3 %copy-start.3 = (bf16[512,512]{1,0:T(8,128)(2,1)S(1)}, bf16[512,512]{1,0:T(8,128)(2,1)}, u32[]{:S(2)}) copy-start(bf16[512,512]{1,0:T(8,128)(2,1)} %param.14) | copy-start | bytes 1572868
  200.5 9.9 %copy-start.5 = (bf16[8,8,8,128]{3,2,1,0:T(8,128)(2,1)}, bf16[8,8,8,128]{3,2,1,0:T(8,128)(2,1)S(1)}, u32[]{:S(2)}) copy-start(bf16[8,8,8,128]{3,2,1,0:T(8,128)(2,1)S(1)} %all-reduce.15) | copy-start | bytes 393220
  201.2 5.6 %collective-permute-start.8 = (bf16[8,1,8,128]{3,2,1,0:T(8,128)(2,1)S(1)}, bf16[8,1,8,128]{3,2,1,0:T(8,128)(2,1)S(1)}, u32[]{:S(2)}, u32[]{:S(2)}) collective-permute-start(bf16[8,1,8,128]{3,2,1,0:T(8,128)(2,1)S(1)} %dynamic-slice_convert_fusion.8), channel_id=1, source_target_pairs={{0,8},{8,0},{16,24},{24,16},{32,40},{40,32},{48,56},{56,48},{64,72... | collective-permute-start | bytes 49160 | tf_op jit(solution)/shard_map/ppermute | solution.py:11
  206.8 6.7 %collective-permute-start.9 = (bf16[8,2,8,128]{3,2,1,0:T(8,128)(2,1)S(1)}, bf16[8,2,8,128]{3,2,1,0:T(8,128)(2,1)S(1)}, u32[]{:S(2)}, u32[]{:S(2)}) collective-permute-start(bf16[8,2,8,128]{3,2,1,0:T(8,128)(2,1)S(1)} %maximum_select_fusion.11), channel_id=1, source_target_pairs={{0,16},{8,24},{16,0},{24,8},{32,48},{40,56},{48,32},{56,40},{64,80... | collective-permute-start | bytes 98312 | tf_op jit(solution)/shard_map/ppermute | solution.py:11
  211.4 7.3 %copy-start.6 = (pred[512,64]{0,1:T(8,128)(4,1)S(1)}, pred[512,64]{0,1:T(8,128)(4,1)}, u32[]{:S(2)}) copy-start(pred[512,64]{0,1:T(8,128)(4,1)} %reshape.248) | copy-start | bytes 98308
  213.5 10.1 %collective-permute-start.10 = (bf16[8,4,8,128]{3,2,1,0:T(8,128)(2,1)S(1)}, bf16[8,4,8,128]{3,2,1,0:T(8,128)(2,1)S(1)}, u32[]{:S(2)}, u32[]{:S(2)}) collective-permute-start(bf16[8,4,8,128]{3,2,1,0:T(8,128)(2,1)S(1)} %maximum_select_fusion.8), channel_id=1, source_target_pairs={{0,32},{8,40},{16,48},{24,56},{32,0},{40,8},{48,16},{56,24},{64,96... | collective-permute-start | bytes 196616 | tf_op jit(solution)/shard_map/ppermute | solution.py:11
  299.3 5.7 %copy-start.9 = (bf16[32,128]{1,0:T(8,128)(2,1)S(1)}, bf16[32,128]{1,0:T(8,128)(2,1)}, u32[]{:S(2)}) copy-start(bf16[32,128]{1,0:T(8,128)(2,1)} %param.17) | copy-start | bytes 24580
  299.3 5.7 %collective-permute-start.11 = (bf16[4,1,8,128]{3,2,1,0:T(8,128)(2,1)S(1)}, bf16[4,1,8,128]{3,2,1,0:T(8,128)(2,1)S(1)}, u32[]{:S(2)}, u32[]{:S(2)}) collective-permute-start(bf16[4,1,8,128]{3,2,1,0:T(8,128)(2,1)S(1)} %dynamic-slice_convert_fusion.14), channel_id=1, source_target_pairs={{0,64},{8,72},{16,80},{24,88},{32,96},{40,104},{48,112},{56,120},{... | collective-permute-start | bytes 24584 | tf_op jit(solution)/shard_map/ppermute | solution.py:11
  302.9 30.2 %copy-start.2 = (bf16[256,512]{1,0:T(8,128)(2,1)S(1)}, bf16[256,512]{1,0:T(8,128)(2,1)}, u32[]{:S(2)}) copy-start(bf16[256,512]{1,0:T(8,128)(2,1)} %param.12) | copy-start | bytes 786436
  304.9 5.5 %collective-permute-start.12 = (bf16[4,1,8,128]{3,2,1,0:T(8,128)(2,1)S(1)}, bf16[4,1,8,128]{3,2,1,0:T(8,128)(2,1)S(1)}, u32[]{:S(2)}, u32[]{:S(2)}) collective-permute-start(bf16[4,1,8,128]{3,2,1,0:T(8,128)(2,1)S(1)} %fusion.14), channel_id=1, source_target_pairs={{0,8},{8,0},{16,24},{24,16},{32,40},{40,32},{48,56},{56,48},{64,72... | collective-permute-start | bytes 24584 | tf_op jit(solution)/shard_map/ppermute | solution.py:11
  310.5 6.7 %collective-permute-start.13 = (bf16[4,2,8,128]{3,2,1,0:T(8,128)(2,1)S(1)}, bf16[4,2,8,128]{3,2,1,0:T(8,128)(2,1)S(1)}, u32[]{:S(2)}, u32[]{:S(2)}) collective-permute-start(bf16[4,2,8,128]{3,2,1,0:T(8,128)(2,1)S(1)} %maximum_select_fusion.14), channel_id=1, source_target_pairs={{0,16},{8,24},{16,0},{24,8},{32,48},{40,56},{48,32},{56,40},{64,80... | collective-permute-start | bytes 49160 | tf_op jit(solution)/shard_map/ppermute | solution.py:11
  317.2 9.7 %collective-permute-start.14 = (bf16[4,4,8,128]{3,2,1,0:T(8,128)(2,1)S(1)}, bf16[4,4,8,128]{3,2,1,0:T(8,128)(2,1)S(1)}, u32[]{:S(2)}, u32[]{:S(2)}) collective-permute-start(bf16[4,4,8,128]{3,2,1,0:T(8,128)(2,1)S(1)} %maximum_select_fusion.12), channel_id=1, source_target_pairs={{0,32},{8,40},{16,48},{24,56},{32,0},{40,8},{48,16},{56,24},{64,96... | collective-permute-start | bytes 98312 | tf_op jit(solution)/shard_map/ppermute | solution.py:11
  326.9 6.2 %collective-permute-start.15 = (bf16[4,8,8,128]{3,2,1,0:T(8,128)(2,1)S(1)}, bf16[4,8,8,128]{3,2,1,0:T(8,128)(2,1)S(1)}, u32[]{:S(2)}, u32[]{:S(2)}) collective-permute-start(bf16[4,8,8,128]{3,2,1,0:T(8,128)(2,1)S(1)} %maximum_select_fusion.9), channel_id=1, source_target_pairs={{0,64},{8,72},{16,80},{24,88},{32,96},{40,104},{48,112},{56,120},{... | collective-permute-start | bytes 196616 | tf_op jit(solution)/shard_map/ppermute | solution.py:11
  362.3 8.9 %all-to-all-start = ((bf16[8,4,1,8,128]{4,3,1,2,0:T(8,128)(2,1)}), bf16[8,4,1,8,128]{4,3,1,2,0:T(8,128)(2,1)S(1)}, u32[]{:S(2)}, u32[]{:S(2)}) async-start(bf16[8,4,1,8,128]{4,3,1,2,0:T(8,128)(2,1)} %stack.10), calls=%async_computation | async-start | bytes 131072 | tf_op jit(solution)/shard_map/all_to_all | solution.py:48
  373.2 6.3 %collective-permute-start.16 = (bf16[4,8,8,128]{3,2,1,0:T(8,128)(2,1)S(1)}, bf16[4,8,8,128]{3,2,1,0:T(8,128)(2,1)}, u32[]{:S(2)}, u32[]{:S(2)}) collective-permute-start(bf16[4,8,8,128]{3,2,1,0:T(8,128)(2,1)S(1)} %fusion), channel_id=1, source_target_pairs={{0,8},{8,0},{16,24},{24,16},{32,40},{40,32},{48,56},{56,48},{64,72... | collective-permute-start | bytes 196616 | tf_op jit(solution)/shard_map/ppermute | solution.py:11
  380.3 7.1 %collective-permute-start.17 = (bf16[4,4,8,128]{3,2,1,0:T(8,128)(2,1)S(1)}, bf16[4,4,8,128]{3,2,1,0:T(8,128)(2,1)S(1)}, u32[]{:S(2)}, u32[]{:S(2)}) collective-permute-start(bf16[4,4,8,128]{3,2,1,0:T(8,128)(2,1)S(1)} %fusion.6), channel_id=1, source_target_pairs={{0,16},{8,24},{16,0},{24,8},{32,48},{40,56},{48,32},{56,40},{64,80... | collective-permute-start | bytes 98312 | tf_op jit(solution)/shard_map/ppermute | solution.py:11
  387.4 9.5 %collective-permute-start.18 = (bf16[4,2,8,128]{3,2,1,0:T(8,128)(2,1)S(1)}, bf16[4,2,8,128]{3,2,1,0:T(8,128)(2,1)S(1)}, u32[]{:S(2)}, u32[]{:S(2)}) collective-permute-start(bf16[4,2,8,128]{3,2,1,0:T(8,128)(2,1)S(1)} %fusion.12), channel_id=1, source_target_pairs={{0,32},{8,40},{16,48},{24,56},{32,0},{40,8},{48,16},{56,24},{64,96... | collective-permute-start | bytes 49160 | tf_op jit(solution)/shard_map/ppermute | solution.py:11
  397.0 5.5 %collective-permute-start.19 = (bf16[4,1,8,128]{3,2,1,0:T(8,128)(2,1)S(1)}, bf16[4,1,8,128]{3,2,1,0:T(8,128)(2,1)S(1)}, u32[]{:S(2)}, u32[]{:S(2)}) collective-permute-start(bf16[4,1,8,128]{3,2,1,0:T(8,128)(2,1)S(1)} %dynamic-slice_convert_fusion.13), channel_id=1, source_target_pairs={{0,64},{8,72},{16,80},{24,88},{32,96},{40,104},{48,112},{56,120},{... | collective-permute-start | bytes 24584 | tf_op jit(solution)/shard_map/ppermute | solution.py:11
  403.1 5.5 %collective-permute-start.20 = (bf16[4,1,8,128]{3,2,1,0:T(8,128)(2,1)S(1)}, bf16[4,1,8,128]{3,2,1,0:T(8,128)(2,1)S(1)}, u32[]{:S(2)}, u32[]{:S(2)}) collective-permute-start(bf16[4,1,8,128]{3,2,1,0:T(8,128)(2,1)S(1)} %get-tuple-element.6), channel_id=1, source_target_pairs={{0,64},{8,72},{16,80},{24,88},{32,96},{40,104},{48,112},{56,120},{... | collective-permute-start | bytes 24584 | tf_op jit(solution)/shard_map/ppermute | solution.py:11
  417.6 6.2 %collective-permute-start.21 = (bf16[8,4,8,128]{3,2,1,0:T(8,128)(2,1)S(1)}, bf16[8,4,8,128]{3,2,1,0:T(8,128)(2,1)S(1)}, u32[]{:S(2)}, u32[]{:S(2)}) collective-permute-start(bf16[8,4,8,128]{3,2,1,0:T(8,128)(2,1)S(1)} %fusion.1), channel_id=1, source_target_pairs={{0,8},{8,0},{16,24},{24,16},{32,40},{40,32},{48,56},{56,48},{64,72... | collective-permute-start | bytes 196616 | tf_op jit(solution)/shard_map/ppermute | solution.py:11
  423.8 7.0 %collective-permute-start.22 = (bf16[8,2,8,128]{3,2,1,0:T(8,128)(2,1)S(1)}, bf16[8,2,8,128]{3,2,1,0:T(8,128)(2,1)S(1)}, u32[]{:S(2)}, u32[]{:S(2)}) collective-permute-start(bf16[8,2,8,128]{3,2,1,0:T(8,128)(2,1)S(1)} %fusion.7), channel_id=1, source_target_pairs={{0,16},{8,24},{16,0},{24,8},{32,48},{40,56},{48,32},{56,40},{64,80... | collective-permute-start | bytes 98312 | tf_op jit(solution)/shard_map/ppermute | solution.py:11
  430.8 9.5 %collective-permute-start.23 = (bf16[8,1,8,128]{3,2,1,0:T(8,128)(2,1)S(1)}, bf16[8,1,8,128]{3,2,1,0:T(8,128)(2,1)S(1)}, u32[]{:S(2)}, u32[]{:S(2)}) collective-permute-start(bf16[8,1,8,128]{3,2,1,0:T(8,128)(2,1)S(1)} %dynamic-slice_convert_fusion.10), channel_id=1, source_target_pairs={{0,32},{8,40},{16,48},{24,56},{32,0},{40,8},{48,16},{56,24},{64,96... | collective-permute-start | bytes 49160 | tf_op jit(solution)/shard_map/ppermute | solution.py:11
  450.7 6.2 %collective-permute-start.24 = (bf16[8,4,8,128]{3,2,1,0:T(8,128)(2,1)S(1)}, bf16[8,4,8,128]{3,2,1,0:T(8,128)(2,1)S(1)}, u32[]{:S(2)}, u32[]{:S(2)}) collective-permute-start(bf16[8,4,8,128]{3,2,1,0:T(8,128)(2,1)S(1)} %fusion.2), channel_id=1, source_target_pairs={{0,8},{8,0},{16,24},{24,16},{32,40},{40,32},{48,56},{56,48},{64,72... | collective-permute-start | bytes 196616 | tf_op jit(solution)/shard_map/ppermute | solution.py:11
  456.9 6.7 %collective-permute-start.25 = (bf16[8,2,8,128]{3,2,1,0:T(8,128)(2,1)S(1)}, bf16[8,2,8,128]{3,2,1,0:T(8,128)(2,1)S(1)}, u32[]{:S(2)}, u32[]{:S(2)}) collective-permute-start(bf16[8,2,8,128]{3,2,1,0:T(8,128)(2,1)S(1)} %fusion.8), channel_id=1, source_target_pairs={{0,16},{8,24},{16,0},{24,8},{32,48},{40,56},{48,32},{56,40},{64,80... | collective-permute-start | bytes 98312 | tf_op jit(solution)/shard_map/ppermute | solution.py:11
  463.6 9.5 %collective-permute-start.26 = (bf16[8,1,8,128]{3,2,1,0:T(8,128)(2,1)S(1)}, bf16[8,1,8,128]{3,2,1,0:T(8,128)(2,1)S(1)}, u32[]{:S(2)}, u32[]{:S(2)}) collective-permute-start(bf16[8,1,8,128]{3,2,1,0:T(8,128)(2,1)S(1)} %dynamic-slice_convert_fusion.9), channel_id=1, source_target_pairs={{0,32},{8,40},{16,48},{24,56},{32,0},{40,8},{48,16},{56,24},{64,96... | collective-permute-start | bytes 49160 | tf_op jit(solution)/shard_map/ppermute | solution.py:11
  473.8 9.5 %collective-permute-start.27 = (bf16[8,1,8,128]{3,2,1,0:T(8,128)(2,1)S(1)}, bf16[8,1,8,128]{3,2,1,0:T(8,128)(2,1)S(1)}, u32[]{:S(2)}, u32[]{:S(2)}) collective-permute-start(bf16[8,1,8,128]{3,2,1,0:T(8,128)(2,1)S(1)} %get-tuple-element.4), channel_id=1, source_target_pairs={{0,32},{8,40},{16,48},{24,56},{32,0},{40,8},{48,16},{56,24},{64,96... | collective-permute-start | bytes 49160 | tf_op jit(solution)/shard_map/ppermute | solution.py:11
  493.8 6.2 %collective-permute-start.28 = (bf16[16,2,8,128]{3,2,1,0:T(8,128)(2,1)S(1)}, bf16[16,2,8,128]{3,2,1,0:T(8,128)(2,1)S(1)}, u32[]{:S(2)}, u32[]{:S(2)}) collective-permute-start(bf16[16,2,8,128]{3,2,1,0:T(8,128)(2,1)S(1)} %fusion.3), channel_id=1, source_target_pairs={{0,8},{8,0},{16,24},{24,16},{32,40},{40,32},{48,56},{56,48},{64,72... | collective-permute-start | bytes 196616 | tf_op jit(solution)/shard_map/ppermute | solution.py:11
  500.1 6.7 %collective-permute-start.29 = (bf16[16,1,8,128]{3,2,1,0:T(8,128)(2,1)S(1)}, bf16[16,1,8,128]{3,2,1,0:T(8,128)(2,1)S(1)}, u32[]{:S(2)}, u32[]{:S(2)}) collective-permute-start(bf16[16,1,8,128]{3,2,1,0:T(8,128)(2,1)S(1)} %dynamic-slice_convert_fusion.7), channel_id=1, source_target_pairs={{0,16},{8,24},{16,0},{24,8},{32,48},{40,56},{48,32},{56,40},{64,80... | collective-permute-start | bytes 98312 | tf_op jit(solution)/shard_map/ppermute | solution.py:11
  518.7 6.2 %collective-permute-start.30 = (bf16[16,2,8,128]{3,2,1,0:T(8,128)(2,1)S(1)}, bf16[16,2,8,128]{3,2,1,0:T(8,128)(2,1)S(1)}, u32[]{:S(2)}, u32[]{:S(2)}) collective-permute-start(bf16[16,2,8,128]{3,2,1,0:T(8,128)(2,1)S(1)} %fusion.4), channel_id=1, source_target_pairs={{0,8},{8,0},{16,24},{24,16},{32,40},{40,32},{48,56},{56,48},{64,72... | collective-permute-start | bytes 196616 | tf_op jit(solution)/shard_map/ppermute | solution.py:11
  524.9 6.7 %collective-permute-start.31 = (bf16[16,1,8,128]{3,2,1,0:T(8,128)(2,1)S(1)}, bf16[16,1,8,128]{3,2,1,0:T(8,128)(2,1)S(1)}, u32[]{:S(2)}, u32[]{:S(2)}) collective-permute-start(bf16[16,1,8,128]{3,2,1,0:T(8,128)(2,1)S(1)} %dynamic-slice_convert_fusion.6), channel_id=1, source_target_pairs={{0,16},{8,24},{16,0},{24,8},{32,48},{40,56},{48,32},{56,40},{64,80... | collective-permute-start | bytes 98312 | tf_op jit(solution)/shard_map/ppermute | solution.py:11
Sparse Core Ops, SparseCore 0:
  67.0 73.0 all-reduce.10
  225.8 72.0 all-reduce.12
